TPU v7x, 32 devices: a whole 2x2x4 slice. The times are simulated.
32 devices in a mesh: ia: 2 (over y), ja: 4 (over x, core), ka: 4 (over z).
Axes of the slice: x: 2, y: 2, z: 4, core: 2. Of those that a mesh axis runs over, the one named last changes fastest.
Arguments:
- tensor: float32 [32, 256, 8192], P('ia', 'ka', 'ja'), may hold values from -6 to 6
- factor_b: float32 [8192, 64], P(('ja', 'ka')), may hold values from -1 to 1
- factor_c: float32 [256, 64], P('ka'), may hold values from -1 to 1
Outputs:
- factor_a: float32 [32, 64], P(('ia', 'ja', 'ka'))
- mode_two: float32 [64, 4, 2048], P(None, 'ja', ('ia', 'ka'))
All inputs are finite; a program needn't handle non-finite values.
Results may differ from a plain program's by a relative error of at most 0.00026.
Values sent between devices are 32-bit elements; how exact they have to be, the bound alone decides.
No kernel may reach another device: no remote copies, remote signals or barrier semaphores. Data moves between devices by JAX's collectives and lax.ppermute only.
A program may use at most 64 MiB of HBM per device.

v0:
```python
import jax
import jax.numpy as jnp
from jax import lax
from jax.sharding import PartitionSpec as P


def body(tensor, factor_b, factor_c):
    highest = lax.Precision.HIGHEST
    factor_rank = factor_c.shape[1]
    row_block = tensor.shape[0]
    column_block = tensor.shape[2]
    local_b = jnp.dot(factor_b.T, factor_b, precision=highest, preferred_element_type=jnp.float32)
    local_c = jnp.dot(factor_c.T, factor_c, precision=highest, preferred_element_type=jnp.float32)
    gram_b = lax.psum(local_b, ("ja", "ka"))
    gram_c = lax.psum(local_c, "ka")
    triangle = jnp.linalg.cholesky(gram_b * gram_c)
    partial_value = jnp.einsum("ikj,kr->rij", tensor, factor_c, precision=highest)
    mode_one = jnp.einsum(
        "rij,jr->ir",
        partial_value,
        lax.all_gather(factor_b, "ka", axis=0, tiled=True),
        precision=highest,
    )
    empty_two = jnp.zeros((factor_rank, column_block), jnp.float32)
    full_sum = lax.psum(mode_one, ("ja", "ka"))
    a_block = jax.scipy.linalg.cho_solve((triangle, True), full_sum.T).T
    row_count = row_block // (lax.axis_size("ja") * lax.axis_size("ka"))
    offset = (lax.axis_index("ja") * lax.axis_size("ka") + lax.axis_index("ka")) * row_count
    a_rows = lax.dynamic_slice_in_dim(a_block, offset, row_count, 0)
    contracted = jnp.einsum("ikj,kr->rij", tensor, factor_c, precision=highest)
    mode_partial = empty_two + jnp.einsum("rij,ir->rj", contracted, a_block, precision=highest)
    reduced = lax.psum_scatter(mode_partial, ("ia", "ka"), scatter_dimension=1, tiled=True)
    return (a_rows, reduced.reshape(factor_rank, 1, reduced.shape[1]))


def solution(mesh):
    placed = (P("ia", "ka", "ja"), P(("ja", "ka"), None), P("ka", None))
    return jax.shard_map(
        body,
        mesh=mesh,
        in_specs=placed,
        out_specs=(P(("ia", "ja", "ka"), None), P(None, "ja", ("ia", "ka"))),
        check_vma=False,
    )
```

profile of v0, /device:TPU:0, one launch (start us, length us, event | category | flops | bytes accessed | tf_op | source)
XLA Modules:
  0.0 229.5 jit_solution(2462762528005702529)
XLA Ops:
  7.2 0.0 copy-start
  7.2 0.0 reduce-scatter.2.cloned.1.call-start
  7.2 17.6 %all_gather.3 = f32[2048,64]{0,1:T(8,128)S(1)} all-gather(f32[512,64]{0,1:T(8,128)} %param.4), channel_id=1, replica_groups=mesh['ia'=2,'ja'=4,'ka'=4] {'ka'}, dimensions={0}, use_global_device_ids=true | all-gather | bytes 655360 | tf_op jit(solution)/shard_map/all_gather | solution.py:21
  24.8 1.2 fusion.13
  26.1 0.0 copy-done
  26.1 0.2 fusion.14
  26.3 11.6 %fusion.6 = f32[64,16,2048]{2,0,1:T(8,128)} fusion(f32[16,64,2048]{2,1,0:T(8,128)} %param.3, f32[64,64]{1,0:T(8,128)S(1)} %copy-done), kind=kOutput, calls=%fused_computation.8 | convolution fusion | flops 1610612736 | bytes 16793600 | tf_op jit(solution)/shard_map/ikj,kr->rij/dot_general | solution.py:17
  37.9 19.8 %psum.22 = f32[64,64]{0,1:T(8,128)S(1)} all-reduce(f32[64,64]{0,1:T(8,128)S(1)} %fusion.14), channel_id=1, replica_groups=mesh['ia'=2,'ja'=4,'ka'=4] {'ka'}, use_global_device_ids=true, to_apply=%region_1.0 | all-reduce | flops 4096 | bytes 32768 | tf_op jit(solution)/shard_map/psum | solution.py:15
  57.7 17.9 %fusion.2 = f32[64,1,16]{2,1,0:T(1,128)S(1)} fusion(f32[64,16,2048]{2,0,1:T(8,128)} %fusion.6, f32[2048,64,1]{0,1,2:T(8,128)S(1)} %bitcast.31), kind=kOutput, calls=%fused_computation.2 | convolution fusion | flops 25165824 | bytes 8916992 | tf_op jit(solution)/shard_map/rij,jr->ir/dot_general | solution.py:18
  75.6 58.2 %all-reduce = (f32[16,64]{0,1:T(8,128)S(1)}, f32[64,64]{0,1:T(8,128)S(1)}) all-reduce(f32[16,64]{0,1:T(8,128)S(1)} %bitcast.33, f32[64,64]{0,1:T(8,128)S(1)} %fusion.13), channel_id=1, replica_groups=mesh['ia'=2,'ja'=4,'ka'=4] {'ja','ka'}, use_global_device_ids=true, to_apply=%region_4.5 | all-reduce | flops 5120 | bytes 40960 | tf_op jit(solution)/shard_map/psum | solution.py:25
  133.8 0.1 copy.7
  133.9 5.8 %cholesky.16 = f32[64,64]{1,0:T(8,128)S(1)} custom-call(f32[64,64]{1,0:T(8,128)S(1)} %fusion.12), custom_call_target="Cholesky" | custom-call | tf_op jit(solution)/shard_map/jit(cholesky)/cholesky | solution.py:16
  139.7 0.6 compare_reduce_fusion
  140.4 0.7 fusion.5
  141.0 4.9 %custom-call.10 = f32[1,64,64]{1,2,0:T(8,128)S(1)} custom-call(f32[1,64,64]{2,1,0:T(8,128)S(1)} %fusion.5), custom_call_target="InvertDiagBlocksLowerTriangular" | custom-call | tf_op jit(solution)/shard_map/jit(_cho_solve)/triangular_solve | solution.py:26
  145.9 0.3 fusion.10
  146.2 0.2 fusion.8
  146.4 0.1 copy.15
  146.5 12.3 %fusion = f32[64,1,2048]{2,1,0:T(1,128)S(1)} fusion(f32[16,64,1]{0,2,1:T(1,128)S(1)} %copy.15, f32[64,16,2048]{2,0,1:T(8,128)} %fusion.6), kind=kOutput, calls=%fused_computation | convolution fusion | flops 25165824 | bytes 8916992 | tf_op jit(solution)/shard_map/rij,ir->rj/dot_general | solution.py:31
  158.8 1.0 copy.25
  159.8 0.0 reduce-scatter.2.cloned.1.call-update
  159.8 0.5 constant_dynamic-slice_fusion
  160.3 60.9 %reduce-scatter.2.cloned.1.call-done = f32[64,256]{1,0:T(8,128)} async-done(((f32[64,2048]{1,0:T(8,128)}), f32[64,256]{1,0:T(8,128)}) %reduce-scatter.2.cloned.1.call-update) | async-done | bytes 65552 | tf_op jit(solution)/shard_map/reduce_scatter | solution.py:32
  221.2 1.5 reshape.20
  (3 shorter events, 0.0 us)
Async XLA Ops:
  7.2 18.9 %copy-start = (f32[64,64]{1,0:T(8,128)S(1)}, f32[64,64]{1,0:T(8,128)}, u32[]{:S(2)}) copy-start(f32[64,64]{1,0:T(8,128)} %param.5) | copy-start | bytes 49156
  7.2 214.0 %reduce-scatter.2.cloned.1.call-start = ((), (), s32[]{:S(2)}) async-start(), calls=%async_computation.1 | async-start | bytes 589824 | tf_op jit(solution)/shard_map/reduce_scatter | solution.py:32
Sparse Core Ops, SparseCore 0:
  159.9 61.2 reduce-scatter.1
where the time goes:
time: 230 us
  blocking collectives  95.6 us (42%)
  waiting for transfers between devices  60.9 us (26%)
  matrix products  43.7 us (19%)
  between operations  14.1 us (6%)
  other arithmetic  12.1 us (5%)
  local copies, waits for them, and re-layouts  3.15 us (1%)
    reduce_scatter x1, waiting for transfers between devices, body(): lax.psum_scatter(mode_partial, ('ia', 'ka'), scatter_dimension=1, tiled=T...  60.9 us
    psum x1, blocking collectives, body(): full_sum = lax.psum(mode_one, ('ja', 'ka'))  58.2 us
    psum x1, blocking collectives, body(): gram_c = lax.psum(local_c, 'ka')  19.8 us
    dot_general x1, matrix products, body(): jnp.einsum('rij,jr->ir', partial_value, lax.all_gather(factor_b, 'ka', ax...  17.9 us
    all_gather x1, blocking collectives, body(): lax.all_gather(factor_b, 'ka', axis=0, tiled=True)  17.6 us
    dot_general x1, matrix products, body(): jnp.einsum('rij,ir->rj', contracted, a_block, precision=highest)  12.3 us
    dot_general x1, matrix products, body(): jnp.einsum('ikj,kr->rij', tensor, factor_c, precision=highest)  11.6 us
    another operation x3, other arithmetic, body(): triangle = jnp.linalg.cholesky(gram_b * gram_c)  6.52 us
  transfers between devices with their start and end apart: 1, of which 1 were waited for; matrix products, arithmetic and copies ran while one was open for 0% of the time, Pallas kernels for 0%

commit v1 on v0

--- a/solution.py
+++ b/solution.py
@@ -15,12 +15,22 @@
     gram_c = lax.psum(local_c, "ka")
     triangle = jnp.linalg.cholesky(gram_b * gram_c)
     partial_value = jnp.einsum("ikj,kr->rij", tensor, factor_c, precision=highest)
-    mode_one = jnp.einsum(
-        "rij,jr->ir",
-        partial_value,
-        lax.all_gather(factor_b, "ka", axis=0, tiled=True),
-        precision=highest,
-    )
+    count, here, rows = (lax.axis_size("ka"), lax.axis_index("ka"), factor_b.shape[0])
+    right = [(i, (i + 1) % count) for i in range(count)]
+    block, total = (factor_b, None)
+    for step in range(count):
+        coming = lax.ppermute(block, "ka", right) if step < count - 1 else None
+        update = jnp.einsum(
+            "rij,jr->ir",
+            lax.dynamic_slice_in_dim(
+                partial_value, (here - step) % count * rows, block.shape[0], axis=2
+            ),
+            block,
+            precision=highest,
+        )
+        total = update if total is None else total + update
+        block = coming
+    mode_one = total
     empty_two = jnp.zeros((factor_rank, column_block), jnp.float32)
     full_sum = lax.psum(mode_one, ("ja", "ka"))
     a_block = jax.scipy.linalg.cho_solve((triangle, True), full_sum.T).T

time: 230 us -> 221 us (0.961)
  blocking collectives: 95.6 us -> 76.5 us
  waiting for transfers between devices: 60.9 us -> 67.7 us
  local copies, waits for them, and re-layouts: 3.15 us -> 7.75 us
  matrix products: 43.7 us -> 39.4 us
  starting transfers between devices: 0.04 us -> 3.38 us
    all_gather x1 -> x0, blocking collectives: 17.6 us -> none  [body(): lax.all_gather(factor_b, 'ka', axis=0, tiled=True)]
    ppermute x0 -> x3, waiting for transfers between devices: none -> 6.83 us  [body(): coming = lax.ppermute(block, 'ka', right) if step < count - 1 else None]
    dynamic_slice x0 -> x1, local copies, waits for them, and re-layouts: none -> 4.59 us  [body(): lax.dynamic_slice_in_dim(partial_value, (here - step) % count * rows, blo...]
    ppermute x0 -> x3, starting transfers between devices: none -> 3.35 us  [body(): coming = lax.ppermute(block, 'ka', right) if step < count - 1 else None]
    dot_general x1 -> x4, matrix products: 17.9 us -> 14.6 us  [body(): jnp.einsum('rij,jr->ir', lax.dynamic_slice_in_dim(partial_value, (here -...]
  transfers between devices with their start and end apart: 1 -> 4, of which waited for: 1 -> 3; matrix products, arithmetic and copies ran while one was open for 0% -> 13% of each run, Pallas kernels for 0% -> 0%
where the time goes in v1:
time: 221 us
  blocking collectives  76.5 us (35%)
  waiting for transfers between devices  67.7 us (31%)
  matrix products  39.4 us (18%)
  between operations  14.2 us (6%)
  other arithmetic  12.1 us (5%)
  local copies, waits for them, and re-layouts  7.75 us (4%)
  starting transfers between devices  3.38 us (2%)
    reduce_scatter x1, waiting for transfers between devices, body(): lax.psum_scatter(mode_partial, ('ia', 'ka'), scatter_dimension=1, tiled=T...  60.8 us
    psum x1, blocking collectives, body(): full_sum = lax.psum(mode_one, ('ja', 'ka'))  58.2 us
    psum x1, blocking collectives, body(): gram_c = lax.psum(local_c, 'ka')  18.3 us
    dot_general x4, matrix products, body(): jnp.einsum('rij,jr->ir', lax.dynamic_slice_in_dim(partial_value, (here -...  14.6 us
    dot_general x1, matrix products, body(): jnp.einsum('rij,ir->rj', contracted, a_block, precision=highest)  12.3 us
    dot_general x1, matrix products, body(): jnp.einsum('ikj,kr->rij', tensor, factor_c, precision=highest)  11.6 us
    ppermute x3, waiting for transfers between devices, body(): coming = lax.ppermute(block, 'ka', right) if step < count - 1 else None  6.83 us
    another operation x3, other arithmetic, body(): triangle = jnp.linalg.cholesky(gram_b * gram_c)  6.52 us
  transfers between devices with their start and end apart: 4, of which 3 were waited for; matrix products, arithmetic and copies ran while one was open for 13% of the time, Pallas kernels for 0%

profile of v1, /device:TPU:0, one launch (start us, length us, event | category | flops | bytes accessed | tf_op | source)
XLA Modules:
  0.0 221.1 jit_solution(8345812106440013657)
XLA Ops:
  7.2 0.0 copy-start
  7.2 0.0 reduce-scatter.2.cloned.1.call-start
  7.2 3.1 %collective-permute-start = (f32[512,64]{0,1:T(8,128)}, f32[512,64]{0,1:T(8,128)S(1)}, u32[]{:S(2)}, u32[]{:S(2)}) collective-permute-start(f32[512,64]{0,1:T(8,128)} %param.4), channel_id=1, source_target_pairs={{0,1},{1,2},{2,3},{3,0},{4,5},{5,6},{6,7},{7,4},{8,9},{9,10},{10,1... | collective-permute-start | bytes 393224 | tf_op jit(solution)/shard_map/ppermute | solution.py:22
  10.3 0.2 fusion.23
  10.6 11.6 %fusion.15 = f32[64,16,2048]{2,0,1:T(8,128)} fusion(f32[16,64,2048]{2,1,0:T(8,128)} %param.3, f32[64,64]{1,0:T(8,128)S(1)} %copy-done), kind=kOutput, calls=%fused_computation.17 | convolution fusion | flops 1610612736 | bytes 16793600 | tf_op jit(solution)/shard_map/ikj,kr->rij/dot_general | solution.py:17
  22.1 18.3 %psum.22 = f32[64,64]{0,1:T(8,128)S(1)} all-reduce(f32[64,64]{0,1:T(8,128)S(1)} %fusion.23), channel_id=1, replica_groups=mesh['ia'=2,'ja'=4,'ka'=4] {'ka'}, use_global_device_ids=true, to_apply=%region_1.0 | all-reduce | flops 4096 | bytes 32768 | tf_op jit(solution)/shard_map/psum | solution.py:15
  40.5 0.0 copy-start.1
  40.5 4.6 %constant_dynamic-slice_fusion.3 = (f32[64,16,512]{2,0,1:T(8,128)S(1)}, f32[64,16,512]{2,0,1:T(8,128)S(1)}, f32[64,16,512]{2,0,1:T(8,128)S(1)}, f32[64,16,512]{2,0,1:T(8,128)S(1)}) fusion(f32[64,16,2048]{2,0,1:T(8,128)} %fusion.15, s32[]{:T(128)S(6)} %select_n.42, s32[]{:T(128)S(6)} %select_n.46, s32[]{:T(128)S(6)} %select_n.44, s32[]{:T(128)S(6)} %select_n.40), kind=kLoop, calls=%fused_computation.33 | loop fusion | bytes 16777232 | tf_op jit(solution)/shard_map/dynamic_slice | solution.py:25
  45.1 3.6 %fusion.8 = f32[64,1,16]{2,1,0:T(1,128)S(1)} fusion(f32[64,16,512]{2,0,1:T(8,128)S(1)} %get-tuple-element.7, f32[512,64,1]{0,1,2:T(8,128)S(1)} %bitcast.41), kind=kOutput, calls=%fused_computation.8 | convolution fusion | flops 6291456 | bytes 2232320 | tf_op jit(solution)/shard_map/rij,jr->ir/dot_general | solution.py:23
  48.8 0.3 fusion.22
  49.0 0.0 collective-permute-done
  49.0 0.2 collective-permute-start.1
  49.3 3.6 %fusion.6 = f32[64,1,16]{2,1,0:T(1,128)S(1)} fusion(f32[64,16,512]{2,0,1:T(8,128)S(1)} %get-tuple-element.4, f32[512,64,1]{0,1,2:T(8,128)S(1)} %bitcast.46), kind=kOutput, calls=%fused_computation.6 | convolution fusion | flops 6291456 | bytes 2232320 | tf_op jit(solution)/shard_map/rij,jr->ir/dot_general | solution.py:23
  52.9 3.7 %collective-permute-done.1 = f32[512,64]{0,1:T(8,128)S(1)} collective-permute-done((f32[512,64]{0,1:T(8,128)S(1)}, f32[512,64]{0,1:T(8,128)S(1)}, u32[]{:S(2)}, u32[]{:S(2)}) %collective-permute-start.1) | collective-permute-done | bytes 131104 | tf_op jit(solution)/shard_map/ppermute | solution.py:22
  56.6 3.6 %fusion.4 = f32[64,1,16]{2,1,0:T(1,128)S(1)} fusion(f32[64,16,512]{2,0,1:T(8,128)S(1)} %get-tuple-element.6, f32[512,64,1]{0,1,2:T(8,128)S(1)} %bitcast.47), kind=kOutput, calls=%fused_computation.4 | convolution fusion | flops 6291456 | bytes 2232320 | tf_op jit(solution)/shard_map/rij,jr->ir/dot_general | solution.py:23
  60.3 3.1 %collective-permute-done.2 = f32[512,64]{0,1:T(8,128)S(1)} collective-permute-done((f32[512,64]{0,1:T(8,128)S(1)}, f32[512,64]{0,1:T(8,128)S(1)}, u32[]{:S(2)}, u32[]{:S(2)}) %collective-permute-start.2) | collective-permute-done | bytes 131104 | tf_op jit(solution)/shard_map/ppermute | solution.py:22
  63.4 3.6 %fusion.2 = f32[64,1,16]{2,1,0:T(1,128)S(1)} fusion(f32[64,16,512]{2,0,1:T(8,128)S(1)} %get-tuple-element.5, f32[512,64,1]{0,1,2:T(8,128)S(1)} %bitcast.48), kind=kOutput, calls=%fused_computation.2 | convolution fusion | flops 6291456 | bytes 2232320 | tf_op jit(solution)/shard_map/rij,jr->ir/dot_general | solution.py:23
  67.1 58.2 %all-reduce = (f32[16,64]{0,1:T(8,128)S(1)}, f32[64,64]{0,1:T(8,128)S(1)}) all-reduce(f32[16,64]{0,1:T(8,128)S(1)} %add_bitcast_fusion, f32[64,64]{0,1:T(8,128)S(1)} %fusion.22), channel_id=1, replica_groups=mesh['ia'=2,'ja'=4,'ka'=4] {'ja','ka'}, use_global_device_ids=true, to_apply=%region_4.5 | all-reduce | flops 5120 | bytes 40960 | tf_op jit(solution)/shard_map/psum | solution.py:35
  125.3 0.1 copy.7
  125.4 5.8 %cholesky.16 = f32[64,64]{1,0:T(8,128)S(1)} custom-call(f32[64,64]{1,0:T(8,128)S(1)} %fusion.21), custom_call_target="Cholesky" | custom-call | tf_op jit(solution)/shard_map/jit(cholesky)/cholesky | solution.py:16
  131.3 0.6 compare_reduce_fusion
  131.9 0.7 fusion.14
  132.6 4.9 %custom-call.10 = f32[1,64,64]{1,2,0:T(8,128)S(1)} custom-call(f32[1,64,64]{2,1,0:T(8,128)S(1)} %fusion.14), custom_call_target="InvertDiagBlocksLowerTriangular" | custom-call | tf_op jit(solution)/shard_map/jit(_cho_solve)/triangular_solve | solution.py:36
  137.5 0.3 fusion.19
  137.7 0.2 fusion.17
  137.9 0.1 copy.25
  138.0 12.3 %fusion = f32[64,1,2048]{2,1,0:T(1,128)S(1)} fusion(f32[16,64,1]{0,2,1:T(1,128)S(1)} %copy.25, f32[64,16,2048]{2,0,1:T(8,128)} %fusion.15), kind=kOutput, calls=%fused_computation | convolution fusion | flops 25165824 | bytes 8916992 | tf_op jit(solution)/shard_map/rij,ir->rj/dot_general | solution.py:41
  150.4 1.0 copy.47
  151.3 0.0 reduce-scatter.2.cloned.1.call-update
  151.4 0.5 constant_dynamic-slice_fusion
  151.9 60.8 %reduce-scatter.2.cloned.1.call-done = f32[64,256]{1,0:T(8,128)} async-done(((f32[64,2048]{1,0:T(8,128)}), f32[64,256]{1,0:T(8,128)}) %reduce-scatter.2.cloned.1.call-update) | async-done | bytes 65552 | tf_op jit(solution)/shard_map/reduce_scatter | solution.py:42
  212.7 1.5 reshape.20
  (7 shorter events, 0.1 us)
Async XLA Ops:
  7.2 3.2 %copy-start = (f32[64,64]{1,0:T(8,128)S(1)}, f32[64,64]{1,0:T(8,128)}, u32[]{:S(2)}) copy-start(f32[64,64]{1,0:T(8,128)} %param.5) | copy-start | bytes 49156
  7.2 205.5 %reduce-scatter.2.cloned.1.call-start = ((), (), s32[]{:S(2)}) async-start(), calls=%async_computation.1 | async-start | bytes 589824 | tf_op jit(solution)/shard_map/reduce_scatter | solution.py:42
  7.2 41.8 %collective-permute-start = (f32[512,64]{0,1:T(8,128)}, f32[512,64]{0,1:T(8,128)S(1)}, u32[]{:S(2)}, u32[]{:S(2)}) collective-permute-start(f32[512,64]{0,1:T(8,128)} %param.4), channel_id=1, source_target_pairs={{0,1},{1,2},{2,3},{3,0},{4,5},{5,6},{6,7},{7,4},{8,9},{9,10},{10,1... | collective-permute-start | bytes 393224 | tf_op jit(solution)/shard_map/ppermute | solution.py:22
  40.5 4.6 %copy-start.1 = (f32[512,64]{0,1:T(8,128)S(1)}, f32[512,64]{0,1:T(8,128)}, u32[]{:S(2)}) copy-start(f32[512,64]{0,1:T(8,128)} %param.4) | copy-start | bytes 393220
  49.0 7.6 %collective-permute-start.1 = (f32[512,64]{0,1:T(8,128)S(1)}, f32[512,64]{0,1:T(8,128)S(1)}, u32[]{:S(2)}, u32[]{:S(2)}) collective-permute-start(f32[512,64]{0,1:T(8,128)S(1)} %collective-permute-done), channel_id=1, source_target_pairs={{0,1},{1,2},{2,3},{3,0},{4,5},{5,6},{6,7},{7,4},{8,9},{9,10},{10,1... | collective-permute-start | bytes 393224 | tf_op jit(solution)/shard_map/ppermute | solution.py:22
  56.6 6.8 %collective-permute-start.2 = (f32[512,64]{0,1:T(8,128)S(1)}, f32[512,64]{0,1:T(8,128)S(1)}, u32[]{:S(2)}, u32[]{:S(2)}) collective-permute-start(f32[512,64]{0,1:T(8,128)S(1)} %collective-permute-done.1), channel_id=1, source_target_pairs={{0,1},{1,2},{2,3},{3,0},{4,5},{5,6},{6,7},{7,4},{8,9},{9,10},{10,1... | collective-permute-start | bytes 393224 | tf_op jit(solution)/shard_map/ppermute | solution.py:22
Sparse Core Ops, SparseCore 0:
  151.5 61.1 reduce-scatter.1
